TPU v7x, 32 devices: a whole 2x2x4 slice. The times are simulated.
32 devices in a mesh: rows: 8 (over z, x), ch: 4 (over y, core).
Axes of the slice: x: 2, y: 2, z: 4, core: 2. Of those that a mesh axis runs over, the one named last changes fastest.
Arguments:
- features: bfloat16 [64, 4096], P('ch', 'rows'), may hold values from -6 to 6
- tiles: bfloat16 [32, 20, 128, 128], P('rows'), may hold values from -0.0625 to 0.0625
- tile_cols: int32 [32, 20], P('rows'), may hold values from 0 to 11, as said below
- needs: int32 [8, 8, 1], P('rows'), may hold values from -1 to 3, as said below
- weights: bfloat16 [4, 64, 64], P(None, 'ch'), may hold values from -0.375 to 0.375
- cotangent: bfloat16 [64, 4096], P('ch', 'rows'), may hold values from -6 to 6
Outputs:
- output: bfloat16 [64, 4096], P('ch', 'rows')
- feature_grad: bfloat16 [64, 4096], P('ch', 'rows')
- weight_grad: float32 [4, 64, 64], P(None, 'ch')
Inputs may be any that keep to these rules, and one draw needn't show every extreme that they name: needs[d, o, s] is a block index of device o, or -1 where unset; row o = d is unset; slot 0 is set for every o other than d; the set entries of one (d, o) differ; some device o has all 1 slots set by every other device. `tile_cols`: the first tile of row block b is its own block (entry b mod 4); an entry v >= 4 names cell v - 4 = 1 o + s with needs[d, o, s] set; every set entry of needs[d] is named by some tile of device d.
All inputs are finite; a program needn't handle non-finite values.
Results may differ from a plain program's by a relative error of at most 0.0055.
Values may be sent and summed in bfloat16 or wider, within the bound.
No kernel may reach another device: no remote copies, remote signals or barrier semaphores. Data moves between devices by JAX's collectives and lax.ppermute only.
A program may use at most 64 MiB of HBM per device.

v0:
```python
import jax
import jax.numpy as jnp
from jax import lax
from jax.sharding import PartitionSpec as P

K = 4


def body(features, tiles, tile_cols, needs, weights, cotangent):
    channels = features.shape[0]
    node_count = features.shape[1]
    blocks = tiles.shape[0]
    per_row = tiles.shape[1]
    block_width = tiles.shape[2]
    slot_count = needs.shape[2]
    shards = lax.axis_size("rows")
    flat_cols = tile_cols.reshape(-1)
    position = lax.axis_index("rows")
    ghost_cell = jnp.clip(flat_cols - blocks, 0, shards * slot_count - 1)
    needed = needs[0].reshape(-1)[ghost_cell]
    remote = ghost_cell // slot_count * blocks + jnp.maximum(needed, 0)
    source_index = jnp.where(flat_cols < blocks, position * blocks + flat_cols, remote)
    extent = blocks * shards

    def gather_source(values):
        return lax.all_gather(values, "rows", axis=1, tiled=True)

    def return_partials(partials):
        return lax.psum_scatter(partials, "rows", scatter_dimension=1, tiled=True)

    def forward_apply(term):
        source = gather_source(term.reshape(channels, blocks, block_width))
        picked = source[:, source_index, :].reshape(channels, blocks, per_row, block_width)
        result = jnp.einsum("crtj,rtij->cri", picked, tiles, preferred_element_type=jnp.float32)
        return result.reshape(channels, node_count)

    def transposed_apply(rounded):
        shaped = rounded.reshape(channels, blocks, block_width)
        contrib = jnp.einsum("cri,rtij->crtj", shaped, tiles, preferred_element_type=jnp.float32)
        contrib = contrib.reshape(channels, blocks * per_row, block_width)
        partials = (
            jnp.zeros((channels, extent, block_width), jnp.float32)
            .at[:, source_index, :]
            .add(contrib)
        )
        return return_partials(partials).reshape(channels, node_count)

    cheb_terms = [features, forward_apply(features).astype(jnp.bfloat16)]
    for degree in range(2, K):
        latest = 2.0 * forward_apply(cheb_terms[-1]) - cheb_terms[-2].astype(jnp.float32)
        cheb_terms.append(latest.astype(jnp.bfloat16))
    stacked = jnp.stack(cheb_terms)
    output = lax.psum_scatter(
        jnp.einsum("kio,kin->on", weights, stacked, preferred_element_type=jnp.float32),
        "ch",
        scatter_dimension=0,
        tiled=True,
    ).astype(jnp.bfloat16)
    grad_out = lax.all_gather(cotangent, "ch", axis=0, tiled=True)
    local_wgrad = jnp.einsum("kin,on->kio", stacked, grad_out, preferred_element_type=jnp.float32)
    weight_grad = lax.psum(local_wgrad, "rows")
    term_grads = jnp.einsum("kio,on->kin", weights, grad_out, preferred_element_type=jnp.float32)
    adjoints = [term_grads[degree] for degree in range(K)]
    for degree in range(K - 1, 1, -1):
        rounded = adjoints[degree].astype(jnp.bfloat16)
        adjoints[degree - 1] = adjoints[degree - 1] + 2.0 * transposed_apply(rounded)
        adjoints[degree - 2] = adjoints[degree - 2] - adjoints[degree]
    last = transposed_apply(adjoints[1].astype(jnp.bfloat16))
    feature_grad = (adjoints[0] + last).astype(jnp.bfloat16)
    return (output, feature_grad, weight_grad)


def solution(mesh):
    placed = (
        P("ch", "rows"),
        P("rows", None, None, None),
        P("rows", None),
        P("rows", None, None),
        P(None, "ch", None),
        P("ch", "rows"),
    )
    return jax.shard_map(
        body,
        mesh=mesh,
        in_specs=placed,
        out_specs=(P("ch", "rows"), P("ch", "rows"), P(None, "ch", None)),
        check_vma=False,
    )
```

profile of v0, /device:TPU:0, one launch (start us, length us, event | category | flops | bytes accessed | tf_op | source)
XLA Modules:
  0.0 292.1 jit_solution(1852419735173445717)
XLA Ops:
  7.2 1.6 fusion.37
  8.9 0.7 broadcast_compare_fusion
  9.5 0.7 add_clamp_fusion
  10.5 6.4 %all_gather.15 = bf16[64,512]{1,0:T(8,128)(2,1)S(1)} all-gather(bf16[16,512]{1,0:T(8,128)(2,1)} %param.11), channel_id=1, replica_groups=mesh['rows'=8,'ch'=4] {'ch'}, dimensions={0}, use_global_device_ids=true | all-gather | bytes 81920 | tf_op jit(solution)/shard_map/all_gather | solution.py:59
  17.6 0.8 fusion.8
  19.6 5.7 %fusion.30 = s32[80]{0:T(128)} fusion(pred[80,1]{0,1:T(4,128)(4,1)S(1)} %lt.31, s32[80,1]{0,1:T(1,128)S(1)} %add.100, s32[80,1]{0,1:T(1,128)S(1)} %min.12, s32[]{:T(128)} %bitcast.3, s32[]{:T(128)} %bitcast.4, s32[]{:T(128)} %bitcast.5, s32[]{:T(128)} %bitcast.6, s32[]{:T(128)} %bitcast.7, s32[]{:T(128)} %bitcast.9, s32[]{:T(128)} %bitcast.8, s32[]{:T(128)} %bitcast.2), kind=kLoop, calls=%fused_computation.64 | loop fusion | flops 1920 | bytes 1072 | tf_op jit(solution)/shard_map/select_n | solution.py:33
  25.2 3.7 %scatter_fusion = f32[16,32,128]{2,0,1:T(8,128)S(1)} fusion(f32[16,32,128]{2,0,1:T(8,128)S(1)} %broadcast.155.clone, s32[80]{0:T(128)} %fusion.30, f32[80,16,128]{2,1,0:T(8,128)S(1)} %bitcast.172), kind=kCustom, calls=%fused_computation.3 | custom fusion | flops 163840 | bytes 1966400 | tf_op jit(solution)/shard_map/scatter-add | solution.py:44
  29.0 0.7 copy-done.2
  29.7 1.4 slice_subtract_fusion
  31.1 0.7 pad_clamp_fusion
  31.8 31.4 %all_gather.12 = bf16[16,32,128]{2,0,1:T(8,128)(2,1)S(1)} all-gather(bf16[16,4,128]{2,0,1:T(8,128)(2,1)S(1)} %copy_bitcast_fusion.1), channel_id=1, replica_groups=mesh['rows'=8,'ch'=4] {'rows'}, dimensions={1}, use_global_device_ids=true | all-gather | bytes 147456 | tf_op jit(solution)/shard_map/all_gather | solution.py:26
  63.2 0.6 gather_fusion
  63.8 0.8 fusion.5
  64.6 30.6 %all_gather.13 = bf16[16,32,128]{2,0,1:T(8,128)(2,1)S(1)} all-gather(bf16[16,4,128]{2,0,1:T(8,128)(2,1)S(1)} %fusion.5), channel_id=1, replica_groups=mesh['rows'=8,'ch'=4] {'rows'}, dimensions={1}, use_global_device_ids=true | all-gather | bytes 147456 | tf_op jit(solution)/shard_map/all_gather | solution.py:26
  96.4 0.6 gather_fusion.1
  97.0 0.8 fusion.3
  98.5 30.5 %all_gather.14 = bf16[16,32,128]{2,0,1:T(8,128)(2,1)S(1)} all-gather(bf16[16,4,128]{2,0,1:T(8,128)(2,1)S(1)} %bitcast.179), channel_id=1, replica_groups=mesh['rows'=8,'ch'=4] {'rows'}, dimensions={1}, use_global_device_ids=true | all-gather | bytes 147456 | tf_op jit(solution)/shard_map/all_gather | solution.py:26
  129.0 1.4 gather_fusion.2
  130.3 1.2 fusion.16
  131.6 3.7 %scatter_fusion.1 = f32[16,32,128]{2,0,1:T(8,128)S(1)} fusion(f32[16,32,128]{2,0,1:T(8,128)S(1)} %broadcast.155.clone.1, s32[80]{0:T(128)} %fusion.30, f32[80,16,128]{2,1,0:T(8,128)S(1)} %bitcast.171), kind=kCustom, calls=%fused_computation.4 | custom fusion | flops 163840 | bytes 1966400 | tf_op jit(solution)/shard_map/scatter-add | solution.py:44
  135.3 0.6 copy-done.3
  136.1 1.7 fusion.1
  138.0 0.9 convolution_bitcast_fusion
  138.9 59.3 %reduce-scatter.9.cloned.1.call-done = f32[16,4,128]{2,0,1:T(8,128)} async-done(((f32[16,32,128]{2,0,1:T(8,128)}), f32[16,4,128]{2,0,1:T(8,128)}) %reduce-scatter.9.cloned.1.call-update) | async-done | bytes 32784 | tf_op jit(solution)/shard_map/reduce_scatter | solution.py:29
  198.3 1.2 fusion.19
  199.5 3.7 %scatter_fusion.2 = f32[16,32,128]{2,0,1:T(8,128)S(1)} fusion(f32[16,32,128]{2,0,1:T(8,128)S(1)} %broadcast.155, s32[80]{0:T(128)} %fusion.30, f32[80,16,128]{2,1,0:T(8,128)S(1)} %bitcast.170), kind=kCustom, calls=%fused_computation.5 | custom fusion | flops 163840 | bytes 1966400 | tf_op jit(solution)/shard_map/scatter-add | solution.py:44
  203.2 0.7 copy-done.1
  203.9 1.0 fusion.6
  205.0 35.8 %psum.7 = f32[4,16,64]{2,1,0:T(8,128)} all-reduce(f32[4,16,64]{2,1,0:T(8,128)S(1)} %fusion.6), channel_id=1, replica_groups=mesh['rows'=8,'ch'=4] {'rows'}, use_global_device_ids=true, to_apply=%region_7.8 | all-reduce | flops 4096 | bytes 32768 | tf_op jit(solution)/shard_map/psum | solution.py:61
  240.8 1.4 convert_element_type.76
  242.1 42.0 %reduce-scatter.11.cloned.1.call-done = f32[16,4,128]{2,0,1:T(8,128)} async-done(((f32[16,32,128]{2,0,1:T(8,128)}), f32[16,4,128]{2,0,1:T(8,128)}) %reduce-scatter.11.cloned.1.call-update) | async-done | bytes 32784 | tf_op jit(solution)/shard_map/reduce_scatter | solution.py:29
  284.2 1.4 fusion.10
  (52 shorter events, 4.3 us)
Async XLA Ops:
  7.2 11.9 %copy-start = (bf16[4,20,128,128]{3,2,1,0:T(8,128)(2,1)S(1)}, bf16[4,20,128,128]{3,2,1,0:T(8,128)(2,1)}, u32[]{:S(2)}) copy-start(bf16[4,20,128,128]{3,2,1,0:T(8,128)(2,1)} %param.7) | copy-start | bytes 7864324
  7.2 123.2 %reduce-scatter.7.cloned.1.call-start = ((), (), s32[]{:S(2)}) async-start(), calls=%async_computation.5 | async-start | bytes 294912 | tf_op jit(solution)/shard_map/reduce_scatter | solution.py:29
  16.9 0.6 copy-start.5
  18.4 0.6 copy-start.4
  19.1 12.7 %copy-start.7 = (bf16[16,512]{1,0:T(8,128)(2,1)S(1)}, bf16[16,512]{1,0:T(8,128)(2,1)}, u32[]{:S(2)}) copy-start(bf16[16,512]{1,0:T(8,128)(2,1)} %param.6) | copy-start | bytes 49156
  28.9 0.7 copy-start.2
  29.7 168.6 %reduce-scatter.9.cloned.1.call-start = ((), (), s32[]{:S(2)}) async-start(), calls=%async_computation.6 | async-start | bytes 294912 | tf_op jit(solution)/shard_map/reduce_scatter | solution.py:29
  135.3 0.7 copy-start.3
  135.3 2.6 copy-start.8
  135.3 2.6 copy-start.10
  135.3 2.6 copy-start.12
  135.3 3.6 %copy-start.6 = (f32[1,16,512]{2,1,0:T(8,128)S(1)}, f32[1,16,512]{2,1,0:T(8,128)}, u32[]{:S(2)}) copy-start(f32[1,16,512]{2,1,0:T(8,128)} %get-tuple-element.3) | copy-start | bytes 98308
  136.0 104.8 %reduce-scatter.5.cloned.1.call-start = ((), (), s32[]{:S(2)}) async-start(), calls=%async_computation.4 | async-start | bytes 163840 | tf_op jit(solution)/shard_map/reduce_scatter | solution.py:53
  137.9 61.6 %copy-start.9 = (bf16[1,16,512]{2,1,0:T(8,128)(2,1)}, bf16[1,16,512]{2,1,0:T(8,128)(2,1)S(1)}, u32[]{:S(2)}) copy-start(bf16[1,16,512]{2,1,0:T(8,128)(2,1)S(1)} %convert_element_type.71) | copy-start | bytes 49156
  137.9 1.0 copy-start.11
  138.8 145.3 %reduce-scatter.11.cloned.1.call-start = ((), (), s32[]{:S(2)}) async-start(), calls=%async_computation.7 | async-start | bytes 294912 | tf_op jit(solution)/shard_map/reduce_scatter | solution.py:29
  203.2 0.7 copy-start.1
Sparse Core Ops, SparseCore 0:
  29.8 62.9 reduce-scatter.6
  136.1 62.0 reduce-scatter.8
  200.7 18.6 reduce-scatter.4
  222.9 61.2 reduce-scatter.10
where the time goes:
time: 293 us; the launch traced here: 292 us
  blocking collectives  135 us (46%)
  waiting for transfers between devices  101 us (34%)
  other arithmetic  23.6 us (8%)
  between operations  14 us (5%)
  local copies, waits for them, and re-layouts  9.28 us (3%)
  matrix products  8.92 us (3%)
    reduce_scatter x3, waiting for transfers between devices, return_partials(): return lax.psum_scatter(partials, 'rows', scatter_dimension=1, tiled=True)  101 us
    all_gather x3, blocking collectives, gather_source(): return lax.all_gather(values, 'rows', axis=1, tiled=True)  92.4 us
    psum x1, blocking collectives, body(): weight_grad = lax.psum(local_wgrad, 'rows')  35.8 us
    scatter-add x3, other arithmetic, transposed_apply(): partials = jnp.zeros((channels, extent, block_width), jnp.float32).at[:,...  11.1 us
    all_gather x1, blocking collectives, body(): grad_out = lax.all_gather(cotangent, 'ch', axis=0, tiled=True)  6.45 us
  transfers between devices with their start and end apart: 4, of which 2 were waited for; matrix products, arithmetic and copies ran while one was open for 6% of the time, Pallas kernels for 0%

commit v1 on v0

--- a/solution.py
+++ b/solution.py
@@ -58,7 +58,10 @@
     ).astype(jnp.bfloat16)
     grad_out = lax.all_gather(cotangent, "ch", axis=0, tiled=True)
     local_wgrad = jnp.einsum("kin,on->kio", stacked, grad_out, preferred_element_type=jnp.float32)
-    weight_grad = lax.psum(local_wgrad, "rows")
+    chips = lax.axis_size("rows")
+    weight_grad = local_wgrad
+    for u in [[(nth, nth ^ j0) for nth in range(chips)] for j0 in (1, 2, 4, 8, 16) if j0 < chips]:
+        weight_grad = weight_grad + lax.ppermute(weight_grad, axis_name="rows", perm=u)
     term_grads = jnp.einsum("kio,on->kin", weights, grad_out, preferred_element_type=jnp.float32)
     adjoints = [term_grads[degree] for degree in range(K)]
     for degree in range(K - 1, 1, -1):

time: 293 us -> 292 us (level)
  blocking collectives: 135 us -> 99.1 us
  waiting for transfers between devices: 101 us -> 132 us
  starting transfers between devices: 0.16 us -> 4.47 us
    psum x1 -> x0, blocking collectives: 35.8 us -> none  [body(): weight_grad = lax.psum(local_wgrad, 'rows')]
    reduce_scatter x3, waiting for transfers between devices: 101 us -> 123 us  [return_partials(): return lax.psum_scatter(partials, 'rows', scatter_dimension=1, tiled=True)]
    ppermute x0 -> x3, waiting for transfers between devices: none -> 8.54 us  [body(): lax.ppermute(weight_grad, axis_name='rows', perm=u)]
    ppermute x0 -> x3, starting transfers between devices: none -> 4.3 us  [body(): lax.ppermute(weight_grad, axis_name='rows', perm=u)]
  transfers between devices with their start and end apart: 4 -> 7, of which waited for: 2 -> 6; matrix products, arithmetic and copies ran while one was open for 6% -> 6% of each run, Pallas kernels for 0% -> 0%
where the time goes in v1:
time: 292 us; the launch traced here: 291 us
  waiting for transfers between devices  132 us (45%)
  blocking collectives  99.1 us (34%)
  other arithmetic  23.4 us (8%)
  between operations  14 us (5%)
  matrix products  8.92 us (3%)
  local copies, waits for them, and re-layouts  8.71 us (3%)
  starting transfers between devices  4.47 us (2%)
    reduce_scatter x3, waiting for transfers between devices, return_partials(): return lax.psum_scatter(partials, 'rows', scatter_dimension=1, tiled=True)  123 us
    all_gather x3, blocking collectives, gather_source(): return lax.all_gather(values, 'rows', axis=1, tiled=True)  92.6 us
    scatter-add x3, other arithmetic, transposed_apply(): partials = jnp.zeros((channels, extent, block_width), jnp.float32).at[:,...  11.1 us
    ppermute x3, waiting for transfers between devices, body(): lax.ppermute(weight_grad, axis_name='rows', perm=u)  8.54 us
    all_gather x1, blocking collectives, body(): grad_out = lax.all_gather(cotangent, 'ch', axis=0, tiled=True)  6.45 us
  transfers between devices with their start and end apart: 7, of which 6 were waited for; matrix products, arithmetic and copies ran while one was open for 6% of the time, Pallas kernels for 0%

profile of v1, /device:TPU:0, one launch (start us, length us, event | category | flops | bytes accessed | tf_op | source)
XLA Modules:
  0.0 290.9 jit_solution(10207715777495857900)
XLA Ops:
  7.2 1.6 fusion.37
  8.8 0.7 broadcast_compare_fusion
  9.5 0.7 add_clamp_fusion
  10.5 6.4 %all_gather.15 = bf16[64,512]{1,0:T(8,128)(2,1)S(1)} all-gather(bf16[16,512]{1,0:T(8,128)(2,1)} %param.11), channel_id=1, replica_groups=mesh['rows'=8,'ch'=4] {'ch'}, dimensions={0}, use_global_device_ids=true | all-gather | bytes 81920 | tf_op jit(solution)/shard_map/all_gather | solution.py:59
  17.6 0.8 fusion.8
  19.6 5.7 %fusion.30 = s32[80]{0:T(128)} fusion(pred[80,1]{0,1:T(4,128)(4,1)S(1)} %lt.31, s32[80,1]{0,1:T(1,128)S(1)} %add.107, s32[80,1]{0,1:T(1,128)S(1)} %min.12, s32[]{:T(128)} %bitcast.3, s32[]{:T(128)} %bitcast.4, s32[]{:T(128)} %bitcast.5, s32[]{:T(128)} %bitcast.6, s32[]{:T(128)} %bitcast.7, s32[]{:T(128)} %bitcast.9, s32[]{:T(128)} %bitcast.8, s32[]{:T(128)} %bitcast.2), kind=kLoop, calls=%fused_computation.64 | loop fusion | flops 1920 | bytes 1072 | tf_op jit(solution)/shard_map/select_n | solution.py:33
  25.3 3.7 %scatter_fusion = f32[16,32,128]{2,0,1:T(8,128)S(1)} fusion(f32[16,32,128]{2,0,1:T(8,128)S(1)} %broadcast.155.clone, s32[80]{0:T(128)} %fusion.30, f32[80,16,128]{2,1,0:T(8,128)S(1)} %bitcast.172), kind=kCustom, calls=%fused_computation.3 | custom fusion | flops 163840 | bytes 1966400 | tf_op jit(solution)/shard_map/scatter-add | solution.py:44
  30.4 31.4 %all_gather.12 = bf16[16,32,128]{2,0,1:T(8,128)(2,1)S(1)} all-gather(bf16[16,4,128]{2,0,1:T(8,128)(2,1)S(1)} %copy_bitcast_fusion.1), channel_id=1, replica_groups=mesh['rows'=8,'ch'=4] {'rows'}, dimensions={1}, use_global_device_ids=true | all-gather | bytes 147456 | tf_op jit(solution)/shard_map/all_gather | solution.py:26
  62.4 0.8 fusion.5
  63.2 30.7 %all_gather.13 = bf16[16,32,128]{2,0,1:T(8,128)(2,1)S(1)} all-gather(bf16[16,4,128]{2,0,1:T(8,128)(2,1)S(1)} %fusion.5), channel_id=1, replica_groups=mesh['rows'=8,'ch'=4] {'rows'}, dimensions={1}, use_global_device_ids=true | all-gather | bytes 147456 | tf_op jit(solution)/shard_map/all_gather | solution.py:26
  94.6 0.8 fusion.3
  96.6 30.5 %all_gather.14 = bf16[16,32,128]{2,0,1:T(8,128)(2,1)S(1)} all-gather(bf16[16,4,128]{2,0,1:T(8,128)(2,1)S(1)} %bitcast.179), channel_id=1, replica_groups=mesh['rows'=8,'ch'=4] {'rows'}, dimensions={1}, use_global_device_ids=true | all-gather | bytes 147456 | tf_op jit(solution)/shard_map/all_gather | solution.py:26
  127.1 1.4 gather_fusion.2
  129.1 1.2 fusion.16
  130.4 3.7 %scatter_fusion.1 = f32[16,32,128]{2,0,1:T(8,128)S(1)} fusion(f32[16,32,128]{2,0,1:T(8,128)S(1)} %broadcast.155.clone.1, s32[80]{0:T(128)} %fusion.30, f32[80,16,128]{2,1,0:T(8,128)S(1)} %bitcast.171), kind=kCustom, calls=%fused_computation.4 | custom fusion | flops 163840 | bytes 1966400 | tf_op jit(solution)/shard_map/scatter-add | solution.py:44
  134.8 1.7 fusion.1
  136.7 0.9 convolution_bitcast_fusion
  137.7 59.3 %reduce-scatter.9.cloned.1.call-done = f32[16,4,128]{2,0,1:T(8,128)} async-done(((f32[16,32,128]{2,0,1:T(8,128)}), f32[16,4,128]{2,0,1:T(8,128)}) %reduce-scatter.9.cloned.1.call-update) | async-done | bytes 32784 | tf_op jit(solution)/shard_map/reduce_scatter | solution.py:29
  197.0 1.2 fusion.19
  198.3 3.7 %scatter_fusion.2 = f32[16,32,128]{2,0,1:T(8,128)S(1)} fusion(f32[16,32,128]{2,0,1:T(8,128)S(1)} %broadcast.155, s32[80]{0:T(128)} %fusion.30, f32[80,16,128]{2,1,0:T(8,128)S(1)} %bitcast.170), kind=kCustom, calls=%fused_computation.5 | custom fusion | flops 163840 | bytes 1966400 | tf_op jit(solution)/shard_map/scatter-add | solution.py:44
  202.0 0.7 copy-done.1
  202.7 1.0 fusion.6
  203.7 1.5 collective-permute-start
  205.2 2.5 collective-permute-done
  207.7 1.4 collective-permute-start.1
  209.2 2.6 collective-permute-done.1
  211.8 1.4 collective-permute-start.2
  213.2 3.4 %collective-permute-done.2 = f32[4,16,64]{2,1,0:T(8,128)S(1)} collective-permute-done((f32[4,16,64]{2,1,0:T(8,128)S(1)}, f32[4,16,64]{2,1,0:T(8,128)S(1)}, u32[]{:S(2)}, u32[]{:S(2)}) %collective-permute-start.2) | collective-permute-done | bytes 16416 | tf_op jit(solution)/shard_map/ppermute | solution.py:64
  217.2 0.9 reduce-scatter.5.cloned.1.call-done
  218.1 1.4 convert_element_type.76
  219.5 63.4 %reduce-scatter.11.cloned.1.call-done = f32[16,4,128]{2,0,1:T(8,128)} async-done(((f32[16,32,128]{2,0,1:T(8,128)}), f32[16,4,128]{2,0,1:T(8,128)}) %reduce-scatter.11.cloned.1.call-update) | async-done | bytes 32784 | tf_op jit(solution)/shard_map/reduce_scatter | solution.py:29
  282.9 1.4 fusion.10
  (62 shorter events, 8.2 us)
Async XLA Ops:
  7.2 11.9 %copy-start = (bf16[4,20,128,128]{3,2,1,0:T(8,128)(2,1)S(1)}, bf16[4,20,128,128]{3,2,1,0:T(8,128)(2,1)}, u32[]{:S(2)}) copy-start(bf16[4,20,128,128]{3,2,1,0:T(8,128)(2,1)} %param.7) | copy-start | bytes 7864324
  7.2 121.9 %reduce-scatter.7.cloned.1.call-start = ((), (), s32[]{:S(2)}) async-start(), calls=%async_computation.5 | async-start | bytes 294912 | tf_op jit(solution)/shard_map/reduce_scatter | solution.py:29
  16.9 0.6 copy-start.6
  18.4 0.7 copy-start.4
  19.1 11.3 %copy-start.8 = (bf16[16,512]{1,0:T(8,128)(2,1)S(1)}, bf16[16,512]{1,0:T(8,128)(2,1)}, u32[]{:S(2)}) copy-start(bf16[16,512]{1,0:T(8,128)(2,1)} %param.6) | copy-start | bytes 49156
  29.0 0.7 copy-start.2
  29.7 167.4 %reduce-scatter.9.cloned.1.call-start = ((), (), s32[]{:S(2)}) async-start(), calls=%async_computation.6 | async-start | bytes 294912 | tf_op jit(solution)/shard_map/reduce_scatter | solution.py:29
  63.2 65.3 %copy-start.5 = (f32[4,16,512]{2,1,0:T(8,128)S(1)}, f32[4,16,512]{2,1,0:T(8,128)}, u32[]{:S(2)}) copy-start(f32[4,16,512]{2,1,0:T(8,128)} %copy-done.4) | copy-start | bytes 393220
  134.1 0.7 copy-start.3
  134.1 2.6 copy-start.9
  134.1 2.6 copy-start.11
  134.1 2.6 copy-start.13
  134.1 3.6 %copy-start.7 = (f32[1,16,512]{2,1,0:T(8,128)S(1)}, f32[1,16,512]{2,1,0:T(8,128)}, u32[]{:S(2)}) copy-start(f32[1,16,512]{2,1,0:T(8,128)} %get-tuple-element.3) | copy-start | bytes 98308
  134.8 83.3 %reduce-scatter.5.cloned.1.call-start = ((), (), s32[]{:S(2)}) async-start(), calls=%async_computation.4 | async-start | bytes 163840 | tf_op jit(solution)/shard_map/reduce_scatter | solution.py:53
  136.7 61.6 %copy-start.10 = (bf16[1,16,512]{2,1,0:T(8,128)(2,1)}, bf16[1,16,512]{2,1,0:T(8,128)(2,1)S(1)}, u32[]{:S(2)}) copy-start(bf16[1,16,512]{2,1,0:T(8,128)(2,1)S(1)} %convert_element_type.71) | copy-start | bytes 49156
  136.7 1.0 copy-start.12
  137.6 145.3 %reduce-scatter.11.cloned.1.call-start = ((), (), s32[]{:S(2)}) async-start(), calls=%async_computation.7 | async-start | bytes 294912 | tf_op jit(solution)/shard_map/reduce_scatter | solution.py:29
  202.0 0.7 copy-start.1
  203.7 4.0 %collective-permute-start = (f32[4,16,64]{2,1,0:T(8,128)S(1)}, f32[4,16,64]{2,1,0:T(8,128)S(1)}, u32[]{:S(2)}, u32[]{:S(2)}) collective-permute-start(f32[4,16,64]{2,1,0:T(8,128)S(1)} %fusion.6), channel_id=1, source_target_pairs={{0,4},{4,0},{8,12},{12,8},{16,20},{20,16},{24,28},{28,24},{1,5},{5... | collective-permute-start | bytes 49160 | tf_op jit(solution)/shard_map/ppermute | solution.py:64
  207.7 4.0 %collective-permute-start.1 = (f32[4,16,64]{2,1,0:T(8,128)S(1)}, f32[4,16,64]{2,1,0:T(8,128)S(1)}, u32[]{:S(2)}, u32[]{:S(2)}) collective-permute-start(f32[4,16,64]{2,1,0:T(8,128)S(1)} %add.116), channel_id=1, source_target_pairs={{0,8},{4,12},{8,0},{12,4},{16,24},{20,28},{24,16},{28,20},{1,9},{5... | collective-permute-start | bytes 49160 | tf_op jit(solution)/shard_map/ppermute | solution.py:64
  211.8 4.8 %collective-permute-start.2 = (f32[4,16,64]{2,1,0:T(8,128)S(1)}, f32[4,16,64]{2,1,0:T(8,128)S(1)}, u32[]{:S(2)}, u32[]{:S(2)}) collective-permute-start(f32[4,16,64]{2,1,0:T(8,128)S(1)} %add.117), channel_id=1, source_target_pairs={{0,16},{4,20},{8,24},{12,28},{16,0},{20,4},{24,8},{28,12},{1,17},{... | collective-permute-start | bytes 49160 | tf_op jit(solution)/shard_map/ppermute | solution.py:64
Sparse Core Ops, SparseCore 0:
  29.8 63.0 reduce-scatter.6
  134.9 62.0 reduce-scatter.8
  199.5 18.6 reduce-scatter.4
  221.7 61.1 reduce-scatter.10
